TPU v7x, 32 devices: a whole 2x2x4 slice. The times are simulated.
32 devices in a mesh: row: 8 (over y, x, core), col: 4 (over z).
Axes of the slice: x: 2, y: 2, z: 4, core: 2. Of those that a mesh axis runs over, the one named last changes fastest.
Arguments:
- chol: float32 [12288, 640], P(('row', 'col')), may hold values from -6 to 6
- eps_occ: float32 [48], replicated, may hold values from -2 to -0.5
- eps_vir: float32 [256], replicated, may hold values from 0.3 to 3
Outputs:
- work: float32 [12288, 640], P(('row', 'col'))
- energies: float32 [2], replicated
All inputs are finite; a program needn't handle non-finite values.
Results may differ from a plain program's by a relative error of at most 0.00013.
Values sent between devices are 32-bit elements; how exact they have to be, the bound alone decides.
A program may use at most 192 MiB of HBM per device.

v0:
```python
import jax
import jax.numpy as jnp
from jax import lax
from jax.sharding import PartitionSpec as P

ITERS = 2


def shards(chol, eps_occ, eps_vir):
    n_row = lax.axis_size("row")
    n_col = lax.axis_size("col")
    row_index = lax.axis_index("row")
    col_index = lax.axis_index("col")
    shard = chol.shape[0]
    width = chol.shape[1]
    occupied = eps_occ.shape[0]
    virtual = eps_vir.shape[0]
    shard_virtuals = shard // occupied
    block_virtuals = n_col * shard_virtuals
    total = virtual * occupied
    row_vir = lax.dynamic_slice_in_dim(eps_vir, row_index * block_virtuals, block_virtuals, 0)
    row_pair = row_vir[:, None] - eps_occ[None, :]
    col_vir = lax.dynamic_slice_in_dim(
        eps_vir.reshape(n_row, block_virtuals), col_index * shard_virtuals, shard_virtuals, 1
    ).reshape(n_row * shard_virtuals)
    col_pair = col_vir[:, None] - eps_occ[None, :]
    chol_cols = lax.all_gather(
        chol.reshape(shard_virtuals, occupied, width), "row", axis=0, tiled=True
    )
    work = jnp.zeros_like(chol)
    sums = []
    for step in range(ITERS):
        factor = chol + work
        rows_factor = lax.all_gather(factor, "col", axis=0, tiled=True)
        piece = lax.all_gather(
            factor.reshape(shard_virtuals, occupied, width), "row", axis=0, tiled=True
        )
        count = piece.shape[0]
        product = lax.dot_general(
            rows_factor,
            piece.reshape(count * occupied, width),
            (((1,), (1,)), ((), ())),
            precision=lax.Precision.HIGHEST,
            preferred_element_type=jnp.float32,
        )
        direct = product.reshape(block_virtuals, occupied, count, occupied)
        numerator = 2.0 * direct - jnp.transpose(direct, (0, 3, 2, 1))
        denominator = row_pair[:, :, None, None] + col_pair[None, None, :, :]
        tile = (-numerator / (jnp.float32(total) * denominator)).reshape(
            block_virtuals * occupied, count * occupied
        )
        chol_piece = chol_cols.reshape(count * occupied, width)
        partial_value = jnp.dot(
            tile, chol_piece, precision=lax.Precision.HIGHEST, preferred_element_type=jnp.float32
        )
        work = lax.psum_scatter(partial_value, "col", scatter_dimension=0, tiled=True)
        local_sum = jnp.sum(chol * work)
        sums.append(local_sum)
    energies = lax.psum(jnp.stack(sums), ("row", "col"))
    return (work, energies / jnp.float32(total))


def solution(mesh):
    placed = (P(("row", "col"), None), P(), P())
    return jax.shard_map(
        shards,
        mesh=mesh,
        in_specs=placed,
        out_specs=(P(("row", "col"), None), P()),
        check_vma=False,
    )
```

profile of v0, /device:TPU:0, one launch (start us, length us, event | category | flops | bytes accessed | tf_op | source)
XLA Modules:
  0.0 1033.4 jit_solution(1675369494210483209)
XLA Ops:
  7.2 0.0 all-gather.5.cloned.1.call-start
  7.2 0.7 all-gather.5.cloned.1.call-update
  7.9 0.0 all-gather.7.cloned.1.call-start
  7.9 2.5 copy.8
  10.4 0.0 all-gather.7.cloned.1.call-update
  10.4 0.0 reduce-scatter.3.cloned.1.call-start
  10.5 0.8 reshape.90
  11.2 0.8 dynamic_slice.6
  12.0 0.1 constant_dynamic-slice_fusion
  12.1 0.1 sub.46
  12.2 0.7 broadcast_subtract_fusion.1
  12.9 0.7 broadcast_subtract_fusion
  13.6 75.1 %all-gather.5.cloned.1.call-done = f32[1536,640]{1,0:T(8,128)} async-done(((f32[384,640]{1,0:T(8,128)}), f32[1536,640]{1,0:T(8,128)}) %all-gather.5.cloned.1.call-update) | async-done | bytes 3932176 | tf_op jit(solution)/shard_map/all_gather | solution.py:34
  88.7 53.0 %all-gather.7.cloned.1.call-done = f32[64,48,640]{2,0,1:T(8,128)} async-done(((f32[8,48,640]{2,0,1:T(8,128)}), f32[64,48,640]{2,0,1:T(8,128)}) %all-gather.7.cloned.1.call-update) | async-done | bytes 7864336 | tf_op jit(solution)/shard_map/all_gather | solution.py:35
  141.7 94.6 %fusion.6 = f32[32,48,64,48]{2,1,3,0:T(8,128)} fusion(f32[32,48,640,1]{2,1,3,0:T(8,128)} %bitcast.47, f32[64,48,640]{2,0,1:T(8,128)} %all-gather.7.cloned.1.call-done), kind=kOutput, calls=%fused_computation.11 | convolution fusion | flops 36238786560 | bytes 30670848 | tf_op jit(solution)/shard_map/dot_general | solution.py:39
  236.3 38.2 %fusion.3 = f32[32,48,64,48]{2,3,1,0:T(8,128)} fusion(f32[32,48,64,48]{2,1,3,0:T(8,128)} %fusion.6, f32[64,48]{0,1:T(8,128)S(1)} %broadcast_subtract_fusion, f32[32,48]{1,0:T(8,128)S(1)} %broadcast_subtract_fusion.1), kind=kLoop, calls=%fused_computation.5 | loop fusion | flops 28311552 | bytes 37767168 | tf_op jit(solution)/shard_map/div | solution.py:49
  274.5 43.4 %copy.10 = f32[32,48,64,48]{3,2,1,0:T(8,128)} copy(f32[32,48,64,48]{2,3,1,0:T(8,128)} %fusion.3) | data formatting | bytes 37748736 | tf_op jit(solution)/shard_map/div | solution.py:49
  317.9 47.0 %reshape.91 = f32[1536,3072]{1,0:T(8,128)} reshape(f32[32,48,64,48]{3,2,1,0:T(8,128)} %copy.10) | data formatting | bytes 37748736 | tf_op jit(solution)/shard_map/reshape | solution.py:49
  364.9 7.8 copy.11
  372.7 0.0 copy-start.1
  372.7 3.0 copy-done.1
  375.7 0.0 copy-start
  375.7 54.5 %fusion.8 = f32[1536,640]{1,0:T(8,128)} fusion(f32[1536,3072]{1,0:T(8,128)} %reshape.91, f32[3072,640]{1,0:T(8,128)S(1)} %bitcast.45), kind=kOutput, calls=%fused_computation.20 | convolution fusion | flops 36238786560 | bytes 30670848 | tf_op jit(solution)/shard_map/dot_general | solution.py:53
  430.2 0.0 reduce-scatter.3.cloned.1.call-update
  430.2 0.0 all-gather.9.cloned.1.call-start
  430.2 72.7 %reduce-scatter.3.cloned.1.call-done = f32[384,640]{1,0:T(8,128)} async-done(((f32[1536,640]{1,0:T(8,128)}), f32[384,640]{1,0:T(8,128)}) %reduce-scatter.3.cloned.1.call-update) | async-done | bytes 983056 | tf_op jit(solution)/shard_map/reduce_scatter | solution.py:56
  503.0 0.0 copy-done
  503.0 2.2 add.40
  505.2 0.0 all-gather.9.cloned.1.call-update
  505.2 0.0 all-gather.11.cloned.1.call-start
  505.3 2.5 copy.12
  507.8 0.0 all-gather.11.cloned.1.call-update
  507.8 0.0 reduce-scatter.5.cloned.1.call-start
  507.8 74.4 %all-gather.9.cloned.1.call-done = f32[1536,640]{1,0:T(8,128)} async-done(((f32[384,640]{1,0:T(8,128)}), f32[1536,640]{1,0:T(8,128)}) %all-gather.9.cloned.1.call-update) | async-done | bytes 3932176 | tf_op jit(solution)/shard_map/all_gather | solution.py:34
  582.2 52.2 %all-gather.11.cloned.1.call-done = f32[64,48,640]{2,0,1:T(8,128)} async-done(((f32[8,48,640]{2,0,1:T(8,128)}), f32[64,48,640]{2,0,1:T(8,128)}) %all-gather.11.cloned.1.call-update) | async-done | bytes 7864336 | tf_op jit(solution)/shard_map/all_gather | solution.py:35
  634.5 94.6 %fusion.4 = f32[32,48,64,48]{2,1,3,0:T(8,128)} fusion(f32[32,48,640,1]{2,1,3,0:T(8,128)} %bitcast.48, f32[64,48,640]{2,0,1:T(8,128)} %all-gather.11.cloned.1.call-done), kind=kOutput, calls=%fused_computation.9 | convolution fusion | flops 36238786560 | bytes 30670848 | tf_op jit(solution)/shard_map/dot_general | solution.py:39
  729.1 38.2 %fusion.1 = f32[32,48,64,48]{2,3,1,0:T(8,128)} fusion(f32[32,48,64,48]{2,1,3,0:T(8,128)} %fusion.4, f32[64,48]{0,1:T(8,128)S(1)} %broadcast_subtract_fusion, f32[32,48]{1,0:T(8,128)S(1)} %broadcast_subtract_fusion.1), kind=kLoop, calls=%fused_computation.2 | loop fusion | flops 28311552 | bytes 37767168 | tf_op jit(solution)/shard_map/div | solution.py:49
  767.3 43.4 %copy.14 = f32[32,48,64,48]{3,2,1,0:T(8,128)} copy(f32[32,48,64,48]{2,3,1,0:T(8,128)} %fusion.1) | data formatting | bytes 37748736 | tf_op jit(solution)/shard_map/div | solution.py:49
  810.7 47.0 %reshape.94 = f32[1536,3072]{1,0:T(8,128)} reshape(f32[32,48,64,48]{3,2,1,0:T(8,128)} %copy.14) | data formatting | bytes 37748736 | tf_op jit(solution)/shard_map/reshape | solution.py:49
  857.7 0.0 copy-start.2
  857.7 51.2 %fusion.9 = f32[1536,640]{1,0:T(8,128)} fusion(f32[1536,3072]{1,0:T(8,128)} %reshape.94, f32[3072,640]{1,0:T(8,128)} %bitcast.46), kind=kOutput, calls=%fused_computation.21 | convolution fusion | flops 36238786560 | bytes 30670848 | tf_op jit(solution)/shard_map/dot_general | solution.py:53
  908.9 0.0 reduce-scatter.5.cloned.1.call-update
  908.9 72.8 %reduce-scatter.5.cloned.1.call-done = f32[384,640]{1,0:T(8,128)} async-done(((f32[1536,640]{1,0:T(8,128)}), f32[384,640]{1,0:T(8,128)}) %reduce-scatter.5.cloned.1.call-update) | async-done | bytes 983056 | tf_op jit(solution)/shard_map/reduce_scatter | solution.py:56
  981.7 0.0 copy-done.2
  981.7 2.1 multiply_reduce_fusion.1
  983.8 1.3 pad_maximum_fusion
  985.0 40.6 %psum.7 = f32[2]{0:T(128)S(1)} all-reduce(f32[2]{0:T(128)S(1)} %pad_maximum_fusion), channel_id=1, replica_groups=mesh['row'=8,'col'=4] {'row','col'}, use_global_device_ids=true, to_apply=%region_4.0 | all-reduce | flops 2 | bytes 16 | tf_op jit(solution)/shard_map/psum | solution.py:59
  1025.6 0.5 broadcast_multiply_fusion
Async XLA Ops:
  7.2 81.6 %all-gather.5.cloned.1.call-start = ((), (), s32[]{:S(2)}) async-start(), calls=%async_computation.2 | async-start | bytes 4915200 | tf_op jit(solution)/shard_map/all_gather | solution.py:34
  7.9 133.8 %all-gather.7.cloned.1.call-start = ((), (), s32[]{:S(2)}) async-start(), calls=%async_computation.3 | async-start | bytes 8847360 | tf_op jit(solution)/shard_map/all_gather | solution.py:35
  10.4 492.5 %reduce-scatter.3.cloned.1.call-start = ((), (), s32[]{:S(2)}) async-start(), calls=%async_computation.4 | async-start | bytes 4915200 | tf_op jit(solution)/shard_map/reduce_scatter | solution.py:56
  372.7 3.0 copy-start.1
  375.7 127.3 %copy-start = (f32[384,640]{1,0:T(8,128)S(1)}, f32[384,640]{1,0:T(8,128)}, u32[]{:S(2)}) copy-start(f32[384,640]{1,0:T(8,128)} %param.3) | copy-start | bytes 2949124
  430.2 152.0 %all-gather.9.cloned.1.call-start = ((), (), s32[]{:S(2)}) async-start(), calls=%async_computation.5 | async-start | bytes 4915200 | tf_op jit(solution)/shard_map/all_gather | solution.py:34
  505.2 129.3 %all-gather.11.cloned.1.call-start = ((), (), s32[]{:S(2)}) async-start(), calls=%async_computation.6 | async-start | bytes 8847360 | tf_op jit(solution)/shard_map/all_gather | solution.py:35
  507.8 473.9 %reduce-scatter.5.cloned.1.call-start = ((), (), s32[]{:S(2)}) async-start(), calls=%async_computation.7 | async-start | bytes 4915200 | tf_op jit(solution)/shard_map/reduce_scatter | solution.py:56
  857.7 124.0 %copy-start.2 = (f32[384,640]{1,0:T(8,128)S(1)}, f32[384,640]{1,0:T(8,128)}, u32[]{:S(2)}) copy-start(f32[384,640]{1,0:T(8,128)} %reduce-scatter.3.cloned.1.call-done) | copy-start | bytes 2949124
Sparse Core Ops, SparseCore 0:
  9.5 79.1 all-gather.4
  91.2 50.4 all-gather.6
  430.3 72.6 reduce-scatter.2
  505.4 76.8 all-gather.8
  584.0 50.4 all-gather.10
  909.0 72.6 reduce-scatter.4
where the time goes:
time: 1050 us; the launch traced here: 1030 us
  waiting for transfers between devices  401 us (38%)
  matrix products  295 us (28%)
  local copies, waits for them, and re-layouts  198 us (19%)
  other arithmetic  84 us (8%)
  blocking collectives  40.6 us (4%)
  between operations  14.5 us (1%)
    dot_general x2, matrix products, shards(): lax.dot_general(rows_factor, piece.reshape(count * occupied, width), (((1...  189 us
    all_gather x2, waiting for transfers between devices, shards(): rows_factor = lax.all_gather(factor, 'col', axis=0, tiled=True)  150 us
    reduce_scatter x2, waiting for transfers between devices, shards(): lax.psum_scatter(partial_value, 'col', scatter_dimension=0, tiled=True)  145 us
    dot_general x2, matrix products, shards(): jnp.dot(tile, chol_piece, precision=lax.Precision.HIGHEST, preferred_elem...  106 us
    all_gather x2, waiting for transfers between devices, shards(): lax.all_gather(factor.reshape(shard_virtuals, occupied, width), 'row', ax...  105 us
    reshape x2, local copies, waits for them, and re-layouts, shards(): (-numerator / (jnp.float32(total) * denominator)).reshape(block_virtuals...  94 us
    div x2, local copies, waits for them, and re-layouts, shards(): -numerator / (jnp.float32(total) * denominator)  86.8 us
    div x2, other arithmetic, shards(): -numerator / (jnp.float32(total) * denominator)  76.5 us
  transfers between devices with their start and end apart: 6, of which 6 were waited for; matrix products, arithmetic and copies ran while one was open for 1% of the time, Pallas kernels for 0%

commit v1 on v0

--- a/solution.py
+++ b/solution.py
@@ -31,7 +31,13 @@
     sums = []
     for step in range(ITERS):
         factor = chol + work
-        rows_factor = lax.all_gather(factor, "col", axis=0, tiled=True)
+        peers = lax.axis_size("col")
+        held, blocks = (factor, [factor])
+        for _ in range(peers - 1):
+            held = lax.ppermute(held, "col", [(i, (i + 1) % peers) for i in range(peers)])
+            blocks.insert(0, held)
+        line = jnp.concatenate(blocks, axis=0)
+        rows_factor = jnp.roll(line, (lax.axis_index("col") + 1) * factor.shape[0], axis=0)
         piece = lax.all_gather(
             factor.reshape(shard_virtuals, occupied, width), "row", axis=0, tiled=True
         )

time: 1050 us -> 958 us (0.912)
  waiting for transfers between devices: 401 us -> 282 us
  other arithmetic: 84 us -> 103 us
  matrix products: 295 us -> 307 us
    all_gather x2 -> x0, waiting for transfers between devices: 150 us -> none  [shards(): rows_factor = lax.all_gather(factor, 'col', axis=0, tiled=True)]
    ppermute x0 -> x6, waiting for transfers between devices: none -> 140 us  [shards(): lax.ppermute(held, 'col', [(i, (i + 1) % peers) for i in range(peers)])]
    all_gather x2, waiting for transfers between devices: 105 us -> 0.01 us  [shards(): lax.all_gather(factor.reshape(shard_virtuals, occupied, width), 'row', ax...]
    concatenate x0 -> x2, other arithmetic: none -> 19.1 us  [shards(): jnp.roll(line, (lax.axis_index('col') + 1) * factor.shape[0], axis=0)]
    dot_general x2, matrix products: 189 us -> 202 us  [shards(): lax.dot_general(rows_factor, piece.reshape(count * occupied, width), (((1...]
  transfers between devices with their start and end apart: 6 -> 10, of which waited for: 6 -> 8; matrix products, arithmetic and copies ran while one was open for 1% -> 2% of each run, Pallas kernels for 0% -> 0%
where the time goes in v1:
time: 958 us; the launch traced here: 949 us
  matrix products  307 us (32%)
  waiting for transfers between devices  282 us (29%)
  local copies, waits for them, and re-layouts  198 us (21%)
  other arithmetic  103 us (11%)
  blocking collectives  40.6 us (4%)
  between operations  14 us (1%)
    dot_general x2, matrix products, shards(): lax.dot_general(rows_factor, piece.reshape(count * occupied, width), (((1...  202 us
    reduce_scatter x2, waiting for transfers between devices, shards(): lax.psum_scatter(partial_value, 'col', scatter_dimension=0, tiled=True)  141 us
    ppermute x6, waiting for transfers between devices, shards(): lax.ppermute(held, 'col', [(i, (i + 1) % peers) for i in range(peers)])  140 us
    dot_general x2, matrix products, shards(): jnp.dot(tile, chol_piece, precision=lax.Precision.HIGHEST, preferred_elem...  106 us
    reshape x2, local copies, waits for them, and re-layouts, shards(): (-numerator / (jnp.float32(total) * denominator)).reshape(block_virtuals...  94 us
    div x2, local copies, waits for them, and re-layouts, shards(): -numerator / (jnp.float32(total) * denominator)  86.8 us
    div x2, other arithmetic, shards(): -numerator / (jnp.float32(total) * denominator)  77.1 us
    psum x1, blocking collectives, shards(): energies = lax.psum(jnp.stack(sums), ('row', 'col'))  40.6 us
  transfers between devices with their start and end apart: 10, of which 8 were waited for; matrix products, arithmetic and copies ran while one was open for 2% of the time, Pallas kernels for 0%

profile of v1, /device:TPU:0, one launch (start us, length us, event | category | flops | bytes accessed | tf_op | source)
XLA Modules:
  0.0 949.5 jit_solution(5889486162077719520)
XLA Ops:
  7.2 0.0 all-gather.3.cloned.1.call-start
  7.2 2.5 copy.8
  9.7 0.0 all-gather.3.cloned.1.call-update
  9.7 0.0 reduce-scatter.3.cloned.1.call-start
  9.7 3.1 collective-permute-start
  12.9 24.0 %collective-permute-done = f32[384,640]{1,0:T(8,128)S(1)} collective-permute-done((f32[384,640]{1,0:T(8,128)}, f32[384,640]{1,0:T(8,128)S(1)}, u32[]{:S(2)}, u32[]{:S(2)}) %collective-permute-start) | collective-permute-done | bytes 983072 | tf_op jit(solution)/shard_map/ppermute | solution.py:37
  36.8 0.0 collective-permute-start.1
  36.8 24.7 %collective-permute-done.1 = f32[384,640]{1,0:T(8,128)S(1)} collective-permute-done((f32[384,640]{1,0:T(8,128)S(1)}, f32[384,640]{1,0:T(8,128)S(1)}, u32[]{:S(2)}, u32[]{:S(2)}) %collective-permute-start.1) | collective-permute-done | bytes 983072 | tf_op jit(solution)/shard_map/ppermute | solution.py:37
  61.6 0.8 reshape.90
  62.3 0.8 dynamic_slice.9
  63.1 0.1 constant_dynamic-slice_fusion
  63.1 0.1 sub.49
  63.2 0.7 broadcast_subtract_fusion.1
  64.0 0.7 broadcast_subtract_fusion
  64.7 20.7 %collective-permute-done.2 = f32[384,640]{1,0:T(8,128)S(1)} collective-permute-done((f32[384,640]{1,0:T(8,128)S(1)}, f32[384,640]{1,0:T(8,128)S(1)}, u32[]{:S(2)}, u32[]{:S(2)}) %collective-permute-start.2) | collective-permute-done | bytes 983072 | tf_op jit(solution)/shard_map/ppermute | solution.py:37
  85.4 9.7 %fusion.18 = f32[1536,640]{1,0:T(8,128)} fusion(s32[]{:T(128)S(6)} %select_n.21, f32[384,640]{1,0:T(8,128)S(1)} %collective-permute-done.2, f32[384,640]{1,0:T(8,128)S(1)} %collective-permute-done.1, f32[384,640]{1,0:T(8,128)S(1)} %collective-permute-done, f32[384,640]{1,0:T(8,128)} %param.5), kind=kLoop, calls=%fused_computation.39 | loop fusion | flops 6881280 | bytes 7864324 | tf_op jit(solution)/shard_map/jit(_roll_dynamic)/concatenate | solution.py:40
  95.1 106.9 %fusion.6 = f32[32,48,64,48]{2,1,3,0:T(8,128)} fusion(f32[32,48,640,1]{2,1,3,0:T(8,128)} %bitcast.48, f32[64,48,640]{2,0,1:T(8,128)} %all-gather.3.cloned.1.call-done), kind=kOutput, calls=%fused_computation.27 | convolution fusion | flops 36238786560 | bytes 30670848 | tf_op jit(solution)/shard_map/dot_general | solution.py:45
  202.1 38.6 %fusion.3 = f32[32,48,64,48]{2,3,1,0:T(8,128)} fusion(f32[32,48,64,48]{2,1,3,0:T(8,128)} %fusion.6, f32[64,48]{0,1:T(8,128)S(1)} %broadcast_subtract_fusion, f32[32,48]{1,0:T(8,128)S(1)} %broadcast_subtract_fusion.1), kind=kLoop, calls=%fused_computation.5 | loop fusion | flops 28311552 | bytes 37767168 | tf_op jit(solution)/shard_map/div | solution.py:55
  240.6 43.4 %copy.10 = f32[32,48,64,48]{3,2,1,0:T(8,128)} copy(f32[32,48,64,48]{2,3,1,0:T(8,128)} %fusion.3) | data formatting | bytes 37748736 | tf_op jit(solution)/shard_map/div | solution.py:55
  284.0 47.0 %reshape.91 = f32[1536,3072]{1,0:T(8,128)} reshape(f32[32,48,64,48]{3,2,1,0:T(8,128)} %copy.10) | data formatting | bytes 37748736 | tf_op jit(solution)/shard_map/reshape | solution.py:55
  331.0 7.8 copy.11
  338.8 3.0 copy-done.1
  341.8 54.4 %fusion.22 = f32[1536,640]{1,0:T(8,128)} fusion(f32[1536,3072]{1,0:T(8,128)} %reshape.91, f32[3072,640]{1,0:T(8,128)S(1)} %bitcast.45), kind=kOutput, calls=%fused_computation.50 | convolution fusion | flops 36238786560 | bytes 30670848 | tf_op jit(solution)/shard_map/dot_general | solution.py:59
  396.3 0.0 reduce-scatter.3.cloned.1.call-update
  396.3 0.0 all-gather.5.cloned.1.call-start
  396.3 70.5 %reduce-scatter.3.cloned.1.call-done = f32[384,640]{1,0:T(8,128)} async-done(((f32[1536,640]{1,0:T(8,128)}), f32[384,640]{1,0:T(8,128)}) %reduce-scatter.3.cloned.1.call-update) | async-done | bytes 983056 | tf_op jit(solution)/shard_map/reduce_scatter | solution.py:62
  466.9 1.3 add.53
  468.2 1.2 copy.12
  469.4 0.0 all-gather.5.cloned.1.call-update
  469.4 0.0 reduce-scatter.5.cloned.1.call-start
  469.5 1.4 collective-permute-start.3
  470.9 23.5 %collective-permute-done.3 = f32[384,640]{1,0:T(8,128)S(1)} collective-permute-done((f32[384,640]{1,0:T(8,128)S(1)}, f32[384,640]{1,0:T(8,128)S(1)}, u32[]{:S(2)}, u32[]{:S(2)}) %collective-permute-start.3) | collective-permute-done | bytes 983072 | tf_op jit(solution)/shard_map/ppermute | solution.py:37
  494.4 0.0 collective-permute-start.4
  494.4 24.0 %collective-permute-done.4 = f32[384,640]{1,0:T(8,128)S(1)} collective-permute-done((f32[384,640]{1,0:T(8,128)S(1)}, f32[384,640]{1,0:T(8,128)S(1)}, u32[]{:S(2)}, u32[]{:S(2)}) %collective-permute-start.4) | collective-permute-done | bytes 983072 | tf_op jit(solution)/shard_map/ppermute | solution.py:37
  518.5 0.9 copy-done.3
  519.4 23.3 %collective-permute-done.5 = f32[384,640]{1,0:T(8,128)} collective-permute-done((f32[384,640]{1,0:T(8,128)S(1)}, f32[384,640]{1,0:T(8,128)}, u32[]{:S(2)}, u32[]{:S(2)}) %collective-permute-start.5) | collective-permute-done | bytes 983072 | tf_op jit(solution)/shard_map/ppermute | solution.py:37
  542.7 9.4 fusion.11
  552.1 94.9 %fusion.4 = f32[32,48,64,48]{2,1,3,0:T(8,128)} fusion(f32[32,48,640,1]{2,1,3,0:T(8,128)} %bitcast.47, f32[64,48,640]{2,0,1:T(8,128)} %all-gather.5.cloned.1.call-done), kind=kOutput, calls=%fused_computation.25 | convolution fusion | flops 36238786560 | bytes 30670848 | tf_op jit(solution)/shard_map/dot_general | solution.py:45
  647.1 38.6 %fusion.1 = f32[32,48,64,48]{2,3,1,0:T(8,128)} fusion(f32[32,48,64,48]{2,1,3,0:T(8,128)} %fusion.4, f32[64,48]{0,1:T(8,128)S(1)} %broadcast_subtract_fusion, f32[32,48]{1,0:T(8,128)S(1)} %broadcast_subtract_fusion.1), kind=kLoop, calls=%fused_computation.2 | loop fusion | flops 28311552 | bytes 37767168 | tf_op jit(solution)/shard_map/div | solution.py:55
  685.6 43.4 %copy.14 = f32[32,48,64,48]{3,2,1,0:T(8,128)} copy(f32[32,48,64,48]{2,3,1,0:T(8,128)} %fusion.1) | data formatting | bytes 37748736 | tf_op jit(solution)/shard_map/div | solution.py:55
  729.0 47.0 %reshape.94 = f32[1536,3072]{1,0:T(8,128)} reshape(f32[32,48,64,48]{3,2,1,0:T(8,128)} %copy.14) | data formatting | bytes 37748736 | tf_op jit(solution)/shard_map/reshape | solution.py:55
  776.0 51.2 %fusion.23 = f32[1536,640]{1,0:T(8,128)} fusion(f32[1536,3072]{1,0:T(8,128)} %reshape.94, f32[3072,640]{1,0:T(8,128)} %bitcast.46), kind=kOutput, calls=%fused_computation.51 | convolution fusion | flops 36238786560 | bytes 30670848 | tf_op jit(solution)/shard_map/dot_general | solution.py:59
  827.2 0.0 reduce-scatter.5.cloned.1.call-update
  827.2 70.9 %reduce-scatter.5.cloned.1.call-done = f32[384,640]{1,0:T(8,128)} async-done(((f32[1536,640]{1,0:T(8,128)}), f32[384,640]{1,0:T(8,128)}) %reduce-scatter.5.cloned.1.call-update) | async-done | bytes 983056 | tf_op jit(solution)/shard_map/reduce_scatter | solution.py:62
  898.1 2.1 multiply_reduce_fusion.1
  900.2 1.4 pad_maximum_fusion
  901.6 40.6 %psum.7 = f32[2]{0:T(128)S(1)} all-reduce(f32[2]{0:T(128)S(1)} %pad_maximum_fusion), channel_id=1, replica_groups=mesh['row'=8,'col'=4] {'row','col'}, use_global_device_ids=true, to_apply=%region_4.6 | all-reduce | flops 2 | bytes 16 | tf_op jit(solution)/shard_map/psum | solution.py:65
  942.2 0.5 broadcast_multiply_fusion
  (10 shorter events, 0.0 us)
Async XLA Ops:
  7.2 88.0 %all-gather.3.cloned.1.call-start = ((), (), s32[]{:S(2)}) async-start(), calls=%async_computation.2 | async-start | bytes 8847360 | tf_op jit(solution)/shard_map/all_gather | solution.py:41
  9.7 457.2 %reduce-scatter.3.cloned.1.call-start = ((), (), s32[]{:S(2)}) async-start(), calls=%async_computation.3 | async-start | bytes 4915200 | tf_op jit(solution)/shard_map/reduce_scatter | solution.py:62
  9.7 27.1 %collective-permute-start = (f32[384,640]{1,0:T(8,128)}, f32[384,640]{1,0:T(8,128)S(1)}, u32[]{:S(2)}, u32[]{:S(2)}) collective-permute-start(f32[384,640]{1,0:T(8,128)} %param.5), channel_id=1, source_target_pairs={{0,1},{1,2},{2,3},{3,0},{4,5},{5,6},{6,7},{7,4},{8,9},{9,10},{10,1... | collective-permute-start | bytes 2949128 | tf_op jit(solution)/shard_map/ppermute | solution.py:37
  36.8 24.7 %collective-permute-start.1 = (f32[384,640]{1,0:T(8,128)S(1)}, f32[384,640]{1,0:T(8,128)S(1)}, u32[]{:S(2)}, u32[]{:S(2)}) collective-permute-start(f32[384,640]{1,0:T(8,128)S(1)} %collective-permute-done), channel_id=1, source_target_pairs={{0,1},{1,2},{2,3},{3,0},{4,5},{5,6},{6,7},{7,4},{8,9},{9,10},{10,1... | collective-permute-start | bytes 2949128 | tf_op jit(solution)/shard_map/ppermute | solution.py:37
  61.6 23.9 %collective-permute-start.2 = (f32[384,640]{1,0:T(8,128)S(1)}, f32[384,640]{1,0:T(8,128)S(1)}, u32[]{:S(2)}, u32[]{:S(2)}) collective-permute-start(f32[384,640]{1,0:T(8,128)S(1)} %collective-permute-done.1), channel_id=1, source_target_pairs={{0,1},{1,2},{2,3},{3,0},{4,5},{5,6},{6,7},{7,4},{8,9},{9,10},{10,1... | collective-permute-start | bytes 2949128 | tf_op jit(solution)/shard_map/ppermute | solution.py:37
  338.8 3.0 copy-start.1
  341.8 125.0 %copy-start = (f32[384,640]{1,0:T(8,128)S(1)}, f32[384,640]{1,0:T(8,128)}, u32[]{:S(2)}) copy-start(f32[384,640]{1,0:T(8,128)} %param.5) | copy-start | bytes 2949124
  396.3 155.8 %all-gather.5.cloned.1.call-start = ((), (), s32[]{:S(2)}) async-start(), calls=%async_computation.4 | async-start | bytes 8847360 | tf_op jit(solution)/shard_map/all_gather | solution.py:41
  469.4 428.7 %reduce-scatter.5.cloned.1.call-start = ((), (), s32[]{:S(2)}) async-start(), calls=%async_computation.5 | async-start | bytes 4915200 | tf_op jit(solution)/shard_map/reduce_scatter | solution.py:62
  469.5 25.0 %collective-permute-start.3 = (f32[384,640]{1,0:T(8,128)S(1)}, f32[384,640]{1,0:T(8,128)S(1)}, u32[]{:S(2)}, u32[]{:S(2)}) collective-permute-start(f32[384,640]{1,0:T(8,128)S(1)} %add.53), channel_id=1, source_target_pairs={{0,1},{1,2},{2,3},{3,0},{4,5},{5,6},{6,7},{7,4},{8,9},{9,10},{10,1... | collective-permute-start | bytes 2949128 | tf_op jit(solution)/shard_map/ppermute | solution.py:37
  494.4 24.0 %collective-permute-start.4 = (f32[384,640]{1,0:T(8,128)S(1)}, f32[384,640]{1,0:T(8,128)S(1)}, u32[]{:S(2)}, u32[]{:S(2)}) collective-permute-start(f32[384,640]{1,0:T(8,128)S(1)} %collective-permute-done.3), channel_id=1, source_target_pairs={{0,1},{1,2},{2,3},{3,0},{4,5},{5,6},{6,7},{7,4},{8,9},{9,10},{10,1... | collective-permute-start | bytes 2949128 | tf_op jit(solution)/shard_map/ppermute | solution.py:37
  518.5 0.9 copy-start.3
  519.4 23.3 %collective-permute-start.5 = (f32[384,640]{1,0:T(8,128)S(1)}, f32[384,640]{1,0:T(8,128)}, u32[]{:S(2)}, u32[]{:S(2)}) collective-permute-start(f32[384,640]{1,0:T(8,128)S(1)} %collective-permute-done.4), channel_id=1, source_target_pairs={{0,1},{1,2},{2,3},{3,0},{4,5},{5,6},{6,7},{7,4},{8,9},{9,10},{10,1... | collective-permute-start | bytes 2949128 | tf_op jit(solution)/shard_map/ppermute | solution.py:37
  776.0 122.1 %copy-start.2 = (f32[384,640]{1,0:T(8,128)S(1)}, f32[384,640]{1,0:T(8,128)}, u32[]{:S(2)}) copy-start(f32[384,640]{1,0:T(8,128)} %reduce-scatter.3.cloned.1.call-done) | copy-start | bytes 2949124
Sparse Core Ops, SparseCore 0:
  10.4 54.6 all-gather.2
  396.4 70.3 reduce-scatter.2
  469.6 52.3 all-gather.4
  827.3 70.7 reduce-scatter.4
